TPU v7x, 32 devices: a whole 2x2x4 slice. The times are simulated.
32 devices in a mesh: head: 4 (over x, core), tok: 8 (over z, y).
Axes of the slice: x: 2, y: 2, z: 4, core: 2. Of those that a mesh axis runs over, the one named last changes fastest.
Arguments:
- tokens: bfloat16 [512, 4096], P('tok'), may hold values from -6 to 6
- attn_gain: float32 [4096], replicated, may hold values from 0.5 to 1.5
- q_weight: bfloat16 [4096, 2048], P('tok', 'head'), may hold values from -0.09375 to 0.09375
- k_weight: bfloat16 [4096, 512], P('tok', 'head'), may hold values from -0.09375 to 0.09375
- v_weight: bfloat16 [4096, 512], P('tok', 'head'), may hold values from -0.09375 to 0.09375
- output_matrix: bfloat16 [2048, 4096], P('head', 'tok'), may hold values from -0.125 to 0.125
- key_cache: bfloat16 [64, 256, 512], P('tok', None, 'head'), may hold values from -400 to 400
- value_cache: bfloat16 [64, 256, 512], P('tok', None, 'head'), may hold values from -6 to 6
- cache_lengths: int32 [64], P('tok'), may hold values from 1 to 256
- row_request_index: int32 [8, 64], P('tok'), may hold values from 0 to 7, never falling along the last dimension, each value on 1 to 32 neighbouring positions
- ffn_gain: float32 [4096], replicated, may hold values from 0.5 to 1.5
- router_weight: bfloat16 [4096, 8], replicated, may hold values from -0.09375 to 0.09375
- routes: int32 [512, 2], P('tok'), may hold values from 0 to 7, all different within a row; in each aligned block of 64 rows (0 to 63, 64 to 127, ...) at most 18 rows name the same one
- gate_weight: bfloat16 [8, 4096, 14336], P('tok', None, 'head'), may hold values from -0.09375 to 0.09375
- up_weight: bfloat16 [8, 4096, 14336], P('tok', None, 'head'), may hold values from -0.09375 to 0.09375
- down_weight: bfloat16 [8, 14336, 4096], P('tok', None, 'head'), may hold values from -0.046875 to 0.046875
Outputs:
- layer_out: bfloat16 [512, 4096], P('tok', 'head')
Inputs may be any that keep to these rules, and one draw needn't show every extreme that they name: `row_request_index`: within the rows of one index of tok the request number never falls, every request has 1 to 32 rows, and one has exactly 32. `routes`: the two experts of a row differ; in the rows of one index of tok no expert is named more than 18 times, and that bound is reached.
All inputs are finite; a program needn't handle non-finite values.
Results may differ from a plain program's by a relative error of at most 0.012.
The roundings to bfloat16 on the way count: a program that leaves them out, or rounds other values in their place, can miss the bound.
Values may be sent and summed in bfloat16 or wider, within the bound.
A program may use at most 256 MiB of HBM per device.

v0:
```python
import jax
import jax.numpy as jnp
from jax import lax
from jax.sharding import PartitionSpec as P

D = 4096
HD = 128
Q_HEADS = 16
KV_HEADS = 4
EXPERTS = 8
CAP = 18
epsilon = 1e-05
rope_base = 1000000.0


def rms_norm(values, gain):
    values = values.astype(jnp.float32)
    factor = lax.rsqrt(jnp.mean(values * values, axis=-1, keepdims=True) + epsilon)
    return (values * factor * gain).astype(jnp.bfloat16)


def rotate(values, positions):
    half = values.shape[-1] // 2
    freqs = rope_base ** (-jnp.arange(half, dtype=jnp.float32) * 2.0 / values.shape[-1])
    angles = positions.astype(jnp.float32)[:, None] * freqs[None, :]
    cosine = jnp.concatenate([jnp.cos(angles), jnp.cos(angles)], axis=-1)[:, None, :]
    sine = jnp.concatenate([jnp.sin(angles), jnp.sin(angles)], axis=-1)[:, None, :]
    turned = jnp.concatenate([-values[..., half:], values[..., :half]], axis=-1)
    return values * cosine + turned * sine


def own_lengths(segment, lengths):
    match = segment[:, None] == jnp.arange(lengths.shape[0], dtype=jnp.int32)[None, :]
    return jnp.sum(jnp.where(match, lengths[None, :], 0), axis=1)


def row_positions(segment, lengths):
    count = segment.shape[0]
    order = jnp.arange(count, dtype=jnp.int32)
    before = jnp.sum((segment[None, :] < segment[:, None]).astype(jnp.int32), axis=1)
    return own_lengths(segment, lengths) + order - before


def attend(queries, new_keys, new_values, key_cache, value_cache, segment, lengths):
    count, kv_local, group, size = queries.shape
    requests, slots, _ = key_cache.shape
    keys = jnp.concatenate([key_cache.reshape(requests * slots, kv_local, size), new_keys], axis=0)
    values = jnp.concatenate(
        [value_cache.reshape(requests * slots, kv_local, size), new_values], axis=0
    )
    slot_index = jnp.arange(requests * slots, dtype=jnp.int32)
    slot_request = slot_index // slots
    slot_place = slot_index % slots
    limit = own_lengths(segment, lengths)
    cache_valid = (slot_request[None, :] == segment[:, None]) & (
        slot_place[None, :] < limit[:, None]
    )
    order = jnp.arange(count, dtype=jnp.int32)
    new_valid = (segment[None, :] == segment[:, None]) & (order[None, :] <= order[:, None])
    allowed = jnp.concatenate([cache_valid, new_valid], axis=1)
    scores = jnp.einsum("rhgd,khd->hgrk", queries, keys, preferred_element_type=jnp.float32)
    scores = scores / jnp.sqrt(jnp.float32(size))
    scores = jnp.where(allowed[None, None], scores, jnp.float32(-1e30))
    highest = jnp.max(scores, axis=-1, keepdims=True)
    weights = jnp.exp(scores - highest)
    probs = (weights / jnp.sum(weights, axis=-1, keepdims=True)).astype(jnp.bfloat16)
    result = jnp.einsum("hgrk,khd->rhgd", probs, values, preferred_element_type=jnp.float32)
    return result.astype(jnp.bfloat16).reshape(count, kv_local * group * size)


def slot_table(chosen):
    flat = chosen.reshape(-1)
    onehot = (flat[:, None] == jnp.arange(EXPERTS, dtype=jnp.int32)[None, :]).astype(jnp.int32)
    earlier = jnp.cumsum(onehot, axis=0) - onehot
    place = jnp.sum(earlier * onehot, axis=1)
    return flat * CAP + place


def fill_slots(normed_rows, places):
    copies = normed_rows[jnp.arange(places.shape[0], dtype=jnp.int32) // 2]
    return jnp.zeros((EXPERTS * CAP, normed_rows.shape[1]), jnp.bfloat16).at[places].set(copies)


def gate_shares(normed_rows, router_weight, chosen):
    logits = jnp.dot(normed_rows, router_weight, preferred_element_type=jnp.float32)
    match = chosen[:, :, None] == jnp.arange(EXPERTS, dtype=jnp.int32)[None, None, :]
    picked = jnp.sum(jnp.where(match, logits[:, None, :], jnp.float32(0.0)), axis=-1)
    return jax.nn.sigmoid(picked - picked[:, ::-1])


def shards(
    tokens,
    attn_gain,
    q_weight,
    k_weight,
    v_weight,
    output_matrix,
    key_cache,
    value_cache,
    cache_lengths,
    row_request_index,
    ffn_gain,
    router_weight,
    routes,
    gate_weight,
    up_weight,
    down_weight,
):
    count = tokens.shape[0]
    group = Q_HEADS // KV_HEADS
    normed = rms_norm(tokens, attn_gain)
    q_full, k_full, v_full, o_full = (
        lax.all_gather(q_weight, "tok", axis=0, tiled=True),
        lax.all_gather(k_weight, "tok", axis=0, tiled=True),
        lax.all_gather(v_weight, "tok", axis=0, tiled=True),
        lax.all_gather(output_matrix, "tok", axis=1, tiled=True),
    )
    kv_local = k_full.shape[1] // HD
    queries = jnp.dot(normed, q_full, preferred_element_type=jnp.float32)
    keys_new = jnp.dot(normed, k_full, preferred_element_type=jnp.float32)
    values_new = jnp.dot(normed, v_full, preferred_element_type=jnp.float32)
    segment = row_request_index[0]
    positions = row_positions(segment, cache_lengths)
    queries = rotate(queries.reshape(count, kv_local * group, HD), positions).astype(jnp.bfloat16)
    queries = queries.reshape(count, kv_local, group, HD)
    keys_new = rotate(keys_new.reshape(count, kv_local, HD), positions).astype(jnp.bfloat16)
    values_new = values_new.astype(jnp.bfloat16).reshape(count, kv_local, HD)
    attn = attend(queries, keys_new, values_new, key_cache, value_cache, segment, cache_lengths)
    partial_mix = jnp.dot(attn, o_full, preferred_element_type=jnp.float32)
    mixed = lax.psum(partial_mix, "head")
    hidden_activation = tokens.astype(jnp.float32) + mixed
    normed_ffn = rms_norm(hidden_activation, ffn_gain)
    shares = gate_shares(normed_ffn, router_weight, routes)
    places = slot_table(routes)
    buffer = fill_slots(normed_ffn, places)
    owners = lax.axis_size("tok")
    slices = owners // EXPERTS
    quarter = down_weight.shape[2]
    head_index = lax.axis_index("head")
    outgoing = jnp.broadcast_to(
        buffer.reshape(EXPERTS, 1, CAP, D), (EXPERTS, slices, CAP, D)
    ).reshape(owners, CAP, D)
    arrived = lax.all_to_all(outgoing, "tok", split_axis=0, concat_axis=0, tiled=True)
    active = jnp.einsum("tcd,df->tcf", arrived, gate_weight[0], preferred_element_type=jnp.float32)
    linear = jnp.einsum("tcd,df->tcf", arrived, up_weight[0], preferred_element_type=jnp.float32)
    hidden = (jax.nn.silu(active) * linear).astype(jnp.bfloat16)
    hidden_all = lax.all_gather(hidden, "head", axis=2, tiled=True)
    output = jnp.einsum(
        "tcf,fd->tcd", hidden_all, down_weight[0], preferred_element_type=jnp.float32
    )
    layer_results = output.astype(jnp.bfloat16)
    returned = lax.all_to_all(layer_results, "tok", split_axis=0, concat_axis=0, tiled=True)
    summed = jnp.sum(returned.reshape(EXPERTS, slices, CAP, quarter).astype(jnp.float32), axis=1)
    summed = summed.reshape(EXPERTS * CAP, quarter)
    picked = jnp.take(summed, places, axis=0).reshape(count, 2, quarter)
    mixture = jnp.sum(shares[:, :, None] * picked, axis=1)
    residual = lax.dynamic_slice_in_dim(hidden_activation, head_index * quarter, quarter, 1)
    return (residual + mixture).astype(jnp.bfloat16)


def solution(mesh):
    in_specs = (
        P("tok", None),
        P(),
        P("tok", "head"),
        P("tok", "head"),
        P("tok", "head"),
        P("head", "tok"),
        P("tok", None, "head"),
        P("tok", None, "head"),
        P("tok"),
        P("tok", None),
        P(),
        P(),
        P("tok", None),
        P("tok", None, "head"),
        P("tok", None, "head"),
        P("tok", None, "head"),
    )
    out_specs = P("tok", "head")
    return jax.shard_map(shards, mesh=mesh, in_specs=in_specs, out_specs=out_specs, check_vma=False)
```

profile of v0, /device:TPU:0, one launch (start us, length us, event | category | flops | bytes accessed | tf_op | source)
XLA Modules:
  0.0 441.3 jit_solution(15756063312826419682)
XLA Ops:
  6.5 0.0 all-gather.6.cloned.1.call-start
  6.6 0.7 all-gather.6.cloned.1.call-update
  7.3 0.0 all-gather.8.cloned.1.call-start
  7.3 0.7 all-gather.8.cloned.1.call-update
  8.0 0.0 all-gather.10.cloned.1.call-start
  8.1 0.7 all-gather.10.cloned.1.call-update
  8.8 0.0 all-gather.12.cloned.1.call-start
  8.8 0.5 all-gather.12.cloned.1.call-update
  9.3 0.0 all-reduce.2.cloned.1.call-start
  9.4 0.8 copy.36
  10.2 0.1 reshape.239
  10.3 0.7 broadcast_multiply_fusion
  11.0 0.1 copy.39
  11.1 0.1 mul.162
  11.2 0.1 fusion.38
  11.3 0.2 reduce_window_sum.11
  11.5 0.9 convert_reduce_fusion
  12.4 0.8 select_reduce_fusion.2
  13.2 1.2 fusion.21
  14.4 0.8 fusion.42
  15.3 0.2 multiply_cosine_fusion
  15.5 0.2 compare_and_fusion
  15.7 36.7 %all-gather.6.cloned.1.call-done = bf16[4096,128]{1,0:T(8,128)(2,1)} async-done(((bf16[512,128]{1,0:T(8,128)(2,1)}), bf16[4096,128]{1,0:T(8,128)(2,1)}) %all-gather.6.cloned.1.call-update) | async-done | bytes 1048592 | tf_op jit(solution)/shard_map/all_gather | solution.py:115
  52.4 1.6 fusion.20
  54.0 39.5 %all-gather.8.cloned.1.call-done = bf16[4096,128]{1,0:T(8,128)(2,1)} async-done(((bf16[512,128]{1,0:T(8,128)(2,1)}), bf16[4096,128]{1,0:T(8,128)(2,1)}) %all-gather.8.cloned.1.call-update) | async-done | bytes 1048592 | tf_op jit(solution)/shard_map/all_gather | solution.py:114
  93.4 1.6 fusion.57
  95.0 0.1 fusion.39
  95.1 0.1 pad_maximum_fusion
  95.2 72.5 %all-gather.10.cloned.1.call-done = bf16[4096,512]{1,0:T(8,128)(2,1)} async-done(((bf16[512,512]{1,0:T(8,128)(2,1)}), bf16[4096,512]{1,0:T(8,128)(2,1)}) %all-gather.10.cloned.1.call-update) | async-done | bytes 4194320 | tf_op jit(solution)/shard_map/all_gather | solution.py:113
  167.8 3.1 fusion.55
  170.9 0.1 slice_negate_fusion
  171.0 0.1 maximum_multiply_fusion
  171.2 0.7 fusion.60
  171.9 0.5 fusion.14
  172.3 0.5 fusion.18
  172.9 0.1 copy.34
  172.9 70.0 %all-gather.12.cloned.1.call-done = bf16[512,4096]{1,0:T(8,128)(2,1)} async-done(((bf16[512,512]{1,0:T(8,128)(2,1)}), bf16[512,4096]{1,0:T(8,128)(2,1)}) %all-gather.12.cloned.1.call-update) | async-done | bytes 4194320 | tf_op jit(solution)/shard_map/all_gather | solution.py:116
  243.0 4.0 fusion.33
  247.0 0.0 all-reduce.2.cloned.1.call-update
  247.0 0.0 all-gather.14.cloned.1.call-start
  247.1 0.2 select_reduce_fusion
  247.3 34.1 %all-reduce.2.cloned.1.call-done = f32[64,4096]{1,0:T(8,128)} async-done(((f32[64,4096]{1,0:T(8,128)}), f32[64,4096]{1,0:T(8,128)}) %all-reduce.2.cloned.1.call-update) | async-done | bytes 1048592 | tf_op jit(solution)/shard_map/psum | solution.py:130
  281.4 1.5 multiply_reduce_fusion
  282.9 0.2 multiply_convert_fusion
  283.1 6.2 %scatter_custom_fusion = bf16[144,4096]{1,0:T(8,128)(2,1)} fusion(s32[128]{0:T(128)S(1)} %fusion.52, bf16[64,4096]{1,0:T(8,128)(2,1)S(1)} %multiply_convert_fusion, s32[1024]{0:T(1024)S(1)} %pad_clamp_fusion.1, bf16[]{:T(256)} %constant.104.clone.1), kind=kCustom, calls=%fused_computation.29 | custom fusion | bytes 1179650 | tf_op jit(solution)/shard_map/scatter | solution.py:81
  289.2 1.4 reshape_reshape.3
  290.7 41.9 %all_to_all.10 = bf16[8,18,4096]{2,1,0:T(8,128)(2,1)S(1)} all-to-all(bf16[8,18,4096]{2,1,0:T(8,128)(2,1)S(1)} %reshape_reshape.3), channel_id=1, replica_groups=mesh['head'=4,'tok'=8] {'tok'}, dimensions={0} | all-to-all | bytes 2359296 | tf_op jit(solution)/shard_map/all_to_all | solution.py:143
  332.6 12.5 %fusion.4 = f32[8,18,3584]{2,1,0:T(8,128)S(1)} fusion(bf16[8,18,4096]{2,1,0:T(8,128)(2,1)S(1)} %all_to_all.10, bf16[1,4096,3584]{2,1,0:T(8,128)(2,1)} %param.29), kind=kOutput, calls=%fused_computation.7 | convolution fusion | flops 4227858432 | bytes 32604160 | tf_op jit(solution)/shard_map/tcd,df->tcf/dot_general | solution.py:144
  345.1 13.5 %fusion.9 = bf16[8,18,3584]{2,1,0:T(8,128)(2,1)} fusion(bf16[8,18,4096]{2,1,0:T(8,128)(2,1)S(1)} %all_to_all.10, bf16[1,4096,3584]{2,1,0:T(8,128)(2,1)} %param.30, f32[8,18,3584]{2,1,0:T(8,128)S(1)} %fusion.4), kind=kOutput, calls=%fused_computation.10 | convolution fusion | flops 4230955008 | bytes 33636352 | tf_op jit(solution)/shard_map/tcd,df->tcf/dot_general | solution.py:145
  358.6 0.0 all-gather.14.cloned.1.call-update
  358.6 0.1 reduce_sum.91
  358.8 0.1 copy.37
  358.8 0.1 copy.38
  359.0 40.4 %all-gather.14.cloned.1.call-done = bf16[8,18,14336]{2,1,0:T(8,128)(2,1)} async-done(((bf16[8,18,3584]{2,1,0:T(8,128)(2,1)}), bf16[8,18,14336]{2,1,0:T(8,128)(2,1)}) %all-gather.14.cloned.1.call-update) | async-done | bytes 4128784 | tf_op jit(solution)/shard_map/all_gather | solution.py:147
  399.4 14.7 %fusion.15 = bf16[8,18,1024]{2,1,0:T(8,128)(2,1)} fusion(bf16[8,18,14336]{2,1,0:T(8,128)(2,1)} %all-gather.14.cloned.1.call-done, bf16[1,14336,1024]{2,1,0:T(8,128)(2,1)} %param.31), kind=kOutput, calls=%fused_computation.20 | convolution fusion | flops 4228005888 | bytes 33783808 | tf_op jit(solution)/shard_map/tcf,fd->tcd/dot_general | solution.py:148
  414.1 5.5 %all-to-all-start.1 = ((bf16[8,18,1024]{2,1,0:T(8,128)(2,1)}), bf16[8,18,1024]{2,1,0:T(8,128)(2,1)S(1)}, u32[]{:S(2)}, u32[]{:S(2)}) async-start(bf16[8,18,1024]{2,1,0:T(8,128)(2,1)} %fusion.15), calls=%async_computation.1 | async-start | bytes 786432 | tf_op jit(solution)/shard_map/all_to_all | solution.py:152
  419.6 0.2 fusion.61
  419.9 0.1 copy.35
  420.0 11.7 %all-to-all-done.1 = bf16[8,18,1024]{2,1,0:T(8,128)(2,1)S(1)} async-done(((bf16[8,18,1024]{2,1,0:T(8,128)(2,1)}), bf16[8,18,1024]{2,1,0:T(8,128)(2,1)S(1)}, u32[]{:S(2)}, u32[]{:S(2)}) %all-to-all-start.1) | async-done | bytes 294944 | tf_op jit(solution)/shard_map/all_to_all | solution.py:152
  431.7 0.1 reshape.243
  431.8 0.8 gather_fusion
  432.6 0.3 gather.11
  432.9 0.8 multiply_reduce_fusion.1
  433.8 0.7 add_convert_fusion
  (32 shorter events, 0.3 us)
Async XLA Ops:
  6.5 413.1 %copy-start = (bf16[4096,8]{0,1:T(8,128)(2,1)S(1)}, bf16[4096,8]{0,1:T(8,128)(2,1)}, u32[]{:S(2)}) copy-start(bf16[4096,8]{0,1:T(8,128)(2,1)} %param.27) | copy-start | bytes 196612
  6.5 8.9 %copy-start.5 = (s32[1,64]{1,0:T(1,128)S(1)}, s32[1,64]{1,0:T(1,128)}, u32[]{:S(2)}) copy-start(s32[1,64]{1,0:T(1,128)} %param.25) | copy-start | bytes 772
  6.5 45.8 %copy-start.1 = (bf16[64,4096]{1,0:T(8,128)(2,1)S(1)}, bf16[64,4096]{1,0:T(8,128)(2,1)}, u32[]{:S(2)}) copy-start(bf16[64,4096]{1,0:T(8,128)(2,1)} %param.16) | copy-start | bytes 1572868
  6.5 45.8 %copy-start.2 = (f32[4096]{0:T(1024)S(1)}, f32[4096]{0:T(1024)}, u32[]{:S(2)}) copy-start(f32[4096]{0:T(1024)} %param.17) | copy-start | bytes 49156
  6.5 45.8 %all-gather.6.cloned.1.call-start = ((), (), s32[]{:S(2)}) async-start(), calls=%async_computation.2 | async-start | bytes 1179648 | tf_op jit(solution)/shard_map/all_gather | solution.py:115
  7.3 86.2 %all-gather.8.cloned.1.call-start = ((), (), s32[]{:S(2)}) async-start(), calls=%async_computation.3 | async-start | bytes 1179648 | tf_op jit(solution)/shard_map/all_gather | solution.py:114
  8.0 159.7 %all-gather.10.cloned.1.call-start = ((), (), s32[]{:S(2)}) async-start(), calls=%async_computation.4 | async-start | bytes 4718592 | tf_op jit(solution)/shard_map/all_gather | solution.py:113
  8.8 234.2 %all-gather.12.cloned.1.call-start = ((), (), s32[]{:S(2)}) async-start(), calls=%async_computation.5 | async-start | bytes 4718592 | tf_op jit(solution)/shard_map/all_gather | solution.py:116
  9.3 272.1 %all-reduce.2.cloned.1.call-start = ((), (), s32[]{:S(2)}) async-start(), calls=%async_computation.6 | async-start | bytes 2097152 | tf_op jit(solution)/shard_map/psum | solution.py:130
  95.2 76.0 %copy-start.6 = (bf16[8,256,128]{2,1,0:T(8,128)(2,1)S(1)}, bf16[8,256,128]{2,1,0:T(8,128)(2,1)}, u32[]{:S(2)}) copy-start(bf16[8,256,128]{2,1,0:T(8,128)(2,1)} %param.22) | copy-start | bytes 1572868
  171.2 1.1 copy-start.7
  247.0 35.9 %copy-start.3 = (f32[4096]{0:T(1024)S(1)}, f32[4096]{0:T(1024)}, u32[]{:S(2)}) copy-start(f32[4096]{0:T(1024)} %param.26) | copy-start | bytes 49156
  247.0 152.4 %all-gather.14.cloned.1.call-start = ((), (), s32[]{:S(2)}) async-start(), calls=%async_computation.7 | async-start | bytes 6881280 | tf_op jit(solution)/shard_map/all_gather | solution.py:147
  345.1 13.7 %copy-start.4 = (s32[64,2]{0,1:T(2,128)S(1)}, s32[64,2]{0,1:T(2,128)}, u32[]{:S(2)}) copy-start(s32[64,2]{0,1:T(2,128)} %param.28) | copy-start | bytes 1540
  414.1 17.6 %all-to-all-start.1 = ((bf16[8,18,1024]{2,1,0:T(8,128)(2,1)}), bf16[8,18,1024]{2,1,0:T(8,128)(2,1)S(1)}, u32[]{:S(2)}, u32[]{:S(2)}) async-start(bf16[8,18,1024]{2,1,0:T(8,128)(2,1)} %fusion.15), calls=%async_computation.1 | async-start | bytes 786432 | tf_op jit(solution)/shard_map/all_to_all | solution.py:152
Sparse Core Ops, SparseCore 0:
  9.5 42.8 all-gather.5
  54.5 38.8 all-gather.7
  95.6 72.1 all-gather.9
  169.7 73.2 all-gather.11
  247.1 34.2 all-reduce.1
  358.7 40.6 all-gather.13
where the time goes:
time: 442 us; the launch traced here: 441 us
  waiting for transfers between devices  308 us (70%)
  matrix products  52.4 us (12%)
  blocking collectives  41.9 us (9%)
  between operations  13.8 us (3%)
  local copies, waits for them, and re-layouts  10.5 us (2%)
  other arithmetic  9.38 us (2%)
  starting transfers between devices  5.74 us (1%)
    all_gather x1, waiting for transfers between devices, shards(): lax.all_gather(q_weight, 'tok', axis=0, tiled=True)  72.5 us
    all_gather x1, waiting for transfers between devices, shards(): lax.all_gather(output_matrix, 'tok', axis=1, tiled=True)  70 us
    all_to_all x1, blocking collectives, shards(): lax.all_to_all(outgoing, 'tok', split_axis=0, concat_axis=0, tiled=True)  41.9 us
    all_gather x1, waiting for transfers between devices, shards(): hidden_all = lax.all_gather(hidden, 'head', axis=2, tiled=True)  40.4 us
    all_gather x1, waiting for transfers between devices, shards(): lax.all_gather(k_weight, 'tok', axis=0, tiled=True)  39.5 us
    all_gather x1, waiting for transfers between devices, shards(): lax.all_gather(v_weight, 'tok', axis=0, tiled=True)  36.7 us
    psum x1, waiting for transfers between devices, shards(): mixed = lax.psum(partial_mix, 'head')  34.1 us
    dot_general x1, matrix products, shards(): jnp.einsum('tcf,fd->tcd', hidden_all, down_weight[0], preferred_element_t...  14.7 us
  transfers between devices with their start and end apart: 7, of which 7 were waited for; matrix products, arithmetic and copies ran while one was open for 4% of the time, Pallas kernels for 0%

commit v1 on v0

--- a/solution.py
+++ b/solution.py
@@ -11,6 +11,17 @@
 CAP = 18
 epsilon = 1e-05
 rope_base = 1000000.0
+
+
+def turned_line(x, mesh_axis, along):
+    size = lax.axis_size(mesh_axis)
+    forward = [(i, (i + 1) % size) for i in range(size)]
+    parts = [x]
+    for reach in range(1, size):
+        parts = [lax.ppermute(parts[0], mesh_axis, forward), *parts]
+    full = jnp.concatenate(parts, axis=along)
+    turn = (lax.axis_index(mesh_axis) + 1) * parts[-1].shape[along]
+    return jnp.roll(full, turn, axis=along)
 
 
 def rms_norm(values, gain):
@@ -144,7 +155,7 @@
     active = jnp.einsum("tcd,df->tcf", arrived, gate_weight[0], preferred_element_type=jnp.float32)
     linear = jnp.einsum("tcd,df->tcf", arrived, up_weight[0], preferred_element_type=jnp.float32)
     hidden = (jax.nn.silu(active) * linear).astype(jnp.bfloat16)
-    hidden_all = lax.all_gather(hidden, "head", axis=2, tiled=True)
+    hidden_all = turned_line(hidden, "head", 2)
     output = jnp.einsum(
         "tcf,fd->tcd", hidden_all, down_weight[0], preferred_element_type=jnp.float32
     )

time: 442 us -> 457 us (1.034)
  local copies, waits for them, and re-layouts: 10.5 us -> 27.8 us
    ppermute x0 -> x3, waiting for transfers between devices: none -> 42.2 us  [turned_line(): parts = [lax.ppermute(parts[0], mesh_axis, forward), *parts]]
    all_gather x1 -> x0, waiting for transfers between devices: 40.4 us -> none  [shards(): hidden_all = lax.all_gather(hidden, 'head', axis=2, tiled=True)]
    unnamed x17 -> x26, local copies, waits for them, and re-layouts: 0.81 us -> 16.6 us
  transfers between devices with their start and end apart: 7 -> 9, of which waited for: 7 -> 9; matrix products, arithmetic and copies ran while one was open for 4% -> 4% of each run, Pallas kernels for 0% -> 0%
where the time goes in v1:
time: 457 us; the launch traced here: 456 us
  waiting for transfers between devices  307 us (67%)
  matrix products  51.7 us (11%)
  blocking collectives  41.9 us (9%)
  local copies, waits for them, and re-layouts  27.8 us (6%)
  between operations  13.5 us (3%)
  other arithmetic  10 us (2%)
    all_gather x1, waiting for transfers between devices, shards(): lax.all_gather(q_weight, 'tok', axis=0, tiled=True)  72.5 us
    all_gather x1, waiting for transfers between devices, shards(): lax.all_gather(output_matrix, 'tok', axis=1, tiled=True)  70 us
    ppermute x3, waiting for transfers between devices, turned_line(): parts = [lax.ppermute(parts[0], mesh_axis, forward), *parts]  42.2 us
    all_to_all x1, blocking collectives, shards(): lax.all_to_all(outgoing, 'tok', split_axis=0, concat_axis=0, tiled=True)  41.9 us
    all_gather x1, waiting for transfers between devices, shards(): lax.all_gather(k_weight, 'tok', axis=0, tiled=True)  39.3 us
    all_gather x1, waiting for transfers between devices, shards(): lax.all_gather(v_weight, 'tok', axis=0, tiled=True)  36.1 us
    psum x1, waiting for transfers between devices, shards(): mixed = lax.psum(partial_mix, 'head')  34.2 us
    unnamed x26, local copies, waits for them, and re-layouts  16.6 us
  transfers between devices with their start and end apart: 9, of which 9 were waited for; matrix products, arithmetic and copies ran while one was open for 4% of the time, Pallas kernels for 0%

profile of v1, /device:TPU:0, one launch (start us, length us, event | category | flops | bytes accessed | tf_op | source)
XLA Modules:
  0.0 456.0 jit_solution(1126135301547903132)
XLA Ops:
  6.5 0.7 all-gather.5.cloned.1.call-update
  7.3 0.7 all-gather.7.cloned.1.call-update
  8.1 0.7 all-gather.9.cloned.1.call-update
  8.8 0.5 all-gather.11.cloned.1.call-update
  9.4 0.8 copy.56
  10.1 0.7 broadcast_multiply_fusion
  10.8 0.1 copy.59
  10.9 0.1 mul.165
  11.1 0.1 reshape.239
  11.2 0.1 fusion.41
  11.3 0.2 reduce_window_sum.11
  11.5 0.9 convert_reduce_fusion
  12.4 0.8 select_reduce_fusion.2
  13.2 1.2 fusion.24
  14.4 0.8 fusion.45
  15.3 0.2 multiply_cosine_fusion
  15.5 0.8 compare_and_fusion
  16.3 36.1 %all-gather.5.cloned.1.call-done = bf16[4096,128]{1,0:T(8,128)(2,1)} async-done(((bf16[512,128]{1,0:T(8,128)(2,1)}), bf16[4096,128]{1,0:T(8,128)(2,1)}) %all-gather.5.cloned.1.call-update) | async-done | bytes 1048592 | tf_op jit(solution)/shard_map/all_gather | solution.py:126
  52.4 1.7 fusion.23
  54.1 39.3 %all-gather.7.cloned.1.call-done = bf16[4096,128]{1,0:T(8,128)(2,1)} async-done(((bf16[512,128]{1,0:T(8,128)(2,1)}), bf16[4096,128]{1,0:T(8,128)(2,1)}) %all-gather.7.cloned.1.call-update) | async-done | bytes 1048592 | tf_op jit(solution)/shard_map/all_gather | solution.py:125
  93.4 1.6 fusion.61
  95.1 0.1 pad_maximum_fusion
  95.2 72.5 %all-gather.9.cloned.1.call-done = bf16[4096,512]{1,0:T(8,128)(2,1)} async-done(((bf16[512,512]{1,0:T(8,128)(2,1)}), bf16[4096,512]{1,0:T(8,128)(2,1)}) %all-gather.9.cloned.1.call-update) | async-done | bytes 4194320 | tf_op jit(solution)/shard_map/all_gather | solution.py:124
  167.8 3.1 fusion.59
  170.9 0.1 slice_negate_fusion
  171.0 0.1 maximum_multiply_fusion
  171.2 0.7 fusion.64
  171.9 0.5 fusion.15
  172.3 0.5 fusion.21
  172.9 70.0 %all-gather.11.cloned.1.call-done = bf16[512,4096]{1,0:T(8,128)(2,1)} async-done(((bf16[512,512]{1,0:T(8,128)(2,1)}), bf16[512,4096]{1,0:T(8,128)(2,1)}) %all-gather.11.cloned.1.call-update) | async-done | bytes 4194320 | tf_op jit(solution)/shard_map/all_gather | solution.py:127
  243.0 4.0 fusion.36
  247.0 0.2 select_reduce_fusion
  247.2 34.2 %all-reduce.2.cloned.1.call-done = f32[64,4096]{1,0:T(8,128)} async-done(((f32[64,4096]{1,0:T(8,128)}), f32[64,4096]{1,0:T(8,128)}) %all-reduce.2.cloned.1.call-update) | async-done | bytes 1048592 | tf_op jit(solution)/shard_map/psum | solution.py:141
  281.4 1.5 multiply_reduce_fusion
  282.9 0.2 multiply_convert_fusion
  283.0 6.1 %scatter_custom_fusion = bf16[144,4096]{1,0:T(8,128)(2,1)} fusion(s32[128]{0:T(128)S(1)} %fusion.55, bf16[64,4096]{1,0:T(8,128)(2,1)S(1)} %multiply_convert_fusion, s32[1024]{0:T(1024)S(1)} %pad_clamp_fusion.1, bf16[]{:T(256)} %constant.122.clone.1), kind=kCustom, calls=%fused_computation.36 | custom fusion | bytes 1179650 | tf_op jit(solution)/shard_map/scatter | solution.py:92
  289.2 1.4 reshape_reshape.3
  290.7 41.9 %all_to_all.10 = bf16[8,18,4096]{2,1,0:T(8,128)(2,1)S(1)} all-to-all(bf16[8,18,4096]{2,1,0:T(8,128)(2,1)S(1)} %reshape_reshape.3), channel_id=1, replica_groups=mesh['head'=4,'tok'=8] {'tok'}, dimensions={0} | all-to-all | bytes 2359296 | tf_op jit(solution)/shard_map/all_to_all | solution.py:154
  332.5 12.5 %fusion.4 = f32[8,18,3584]{2,1,0:T(8,128)S(1)} fusion(bf16[8,18,4096]{2,1,0:T(8,128)(2,1)S(1)} %all_to_all.10, bf16[1,4096,3584]{2,1,0:T(8,128)(2,1)} %param.29), kind=kOutput, calls=%fused_computation.7 | convolution fusion | flops 4227858432 | bytes 32604160 | tf_op jit(solution)/shard_map/tcd,df->tcf/dot_general | solution.py:155
  345.1 12.6 %fusion.10 = bf16[8,18,3584]{2,1,0:T(8,128)(2,1)S(1)} fusion(bf16[8,18,4096]{2,1,0:T(8,128)(2,1)S(1)} %all_to_all.10, bf16[1,4096,3584]{2,1,0:T(8,128)(2,1)} %param.30, f32[8,18,3584]{2,1,0:T(8,128)S(1)} %fusion.4), kind=kOutput, calls=%fused_computation.11 | convolution fusion | flops 4230955008 | bytes 33636352 | tf_op jit(solution)/shard_map/tcd,df->tcf/dot_general | solution.py:156
  357.7 0.3 copy.60
  358.1 14.0 %collective-permute-done = bf16[8,18,3584]{2,0,1:T(8,128)(2,1)S(1)} collective-permute-done((bf16[8,18,3584]{2,0,1:T(8,128)(2,1)S(1)}, bf16[8,18,3584]{2,0,1:T(8,128)(2,1)S(1)}, u32[]{:S(2)}, u32[]{:S(2)}) %collective-permute-start) | collective-permute-done | bytes 1032224 | tf_op jit(solution)/shard_map/ppermute | solution.py:21
  372.1 1.0 copy-done.2
  373.1 14.2 %collective-permute-done.1 = bf16[8,18,3584]{2,0,1:T(8,128)(2,1)} collective-permute-done((bf16[8,18,3584]{2,0,1:T(8,128)(2,1)S(1)}, bf16[8,18,3584]{2,0,1:T(8,128)(2,1)}, u32[]{:S(2)}, u32[]{:S(2)}) %collective-permute-start.1) | collective-permute-done | bytes 1032224 | tf_op jit(solution)/shard_map/ppermute | solution.py:21
  387.3 0.1 reduce_sum.91
  387.5 0.1 copy.58
  387.7 14.0 %collective-permute-done.2 = bf16[8,18,3584]{2,0,1:T(8,128)(2,1)} collective-permute-done((bf16[8,18,3584]{2,0,1:T(8,128)(2,1)}, bf16[8,18,3584]{2,0,1:T(8,128)(2,1)}, u32[]{:S(2)}, u32[]{:S(2)}) %collective-permute-start.2) | collective-permute-done | bytes 1032224 | tf_op jit(solution)/shard_map/ppermute | solution.py:21
  401.7 2.6 copy_dynamic-update-slice_fusion.4
  404.3 2.7 copy_dynamic-update-slice_fusion.2
  407.0 1.5 copy_dynamic-update-slice_fusion
  408.5 1.2 constant_dynamic-update-slice_fusion.1
  409.7 2.6 copy_dynamic-update-slice_fusion.5
  412.3 2.7 copy_dynamic-update-slice_fusion.3
  415.0 1.5 copy_dynamic-update-slice_fusion.1
  416.4 1.2 constant_dynamic-update-slice_fusion
  417.7 14.8 %fusion.16 = bf16[8,18,1024]{2,1,0:T(8,128)(2,1)} fusion(bf16[1,14336,1024]{2,1,0:T(8,128)(2,1)} %param.31, bf16[8,18,28672]{2,1,0:T(8,128)(2,1)} %constant_dynamic-update-slice_fusion, s32[]{:T(128)S(6)} %select_n.103), kind=kOutput, calls=%fused_computation.27 | convolution fusion | flops 4228005888 | bytes 35160068 | tf_op jit(solution)/shard_map/tcf,fd->tcd/dot_general | solution.py:159
  432.4 3.5 all-to-all-start.1
  436.0 0.2 fusion.65
  436.3 0.1 copy.55
  436.4 10.4 %all-to-all-done.1 = bf16[8,18,1024]{2,1,0:T(8,128)(2,1)S(1)} async-done(((bf16[8,18,1024]{2,1,0:T(8,128)(2,1)}), bf16[8,18,1024]{2,1,0:T(8,128)(2,1)S(1)}, u32[]{:S(2)}, u32[]{:S(2)}) %all-to-all-start.1) | async-done | bytes 294944 | tf_op jit(solution)/shard_map/all_to_all | solution.py:163
  446.9 0.8 gather_fusion
  447.7 0.3 gather.11
  448.0 0.8 multiply_reduce_fusion.1
  448.8 0.7 add_convert_fusion
  (46 shorter events, 0.8 us)
Async XLA Ops:
  6.5 429.5 %copy-start = (bf16[4096,8]{0,1:T(8,128)(2,1)S(1)}, bf16[4096,8]{0,1:T(8,128)(2,1)}, u32[]{:S(2)}) copy-start(bf16[4096,8]{0,1:T(8,128)(2,1)} %param.27) | copy-start | bytes 196612
  6.5 86.9 %copy-start.1 = (bf16[64,4096]{1,0:T(8,128)(2,1)S(1)}, bf16[64,4096]{1,0:T(8,128)(2,1)}, u32[]{:S(2)}) copy-start(bf16[64,4096]{1,0:T(8,128)(2,1)} %param.16) | copy-start | bytes 1572868
  6.5 86.9 %copy-start.4 = (f32[4096]{0:T(1024)S(1)}, f32[4096]{0:T(1024)}, u32[]{:S(2)}) copy-start(f32[4096]{0:T(1024)} %param.17) | copy-start | bytes 49156
  6.5 45.8 %all-gather.5.cloned.1.call-start = ((), (), s32[]{:S(2)}) async-start(), calls=%async_computation.2 | async-start | bytes 1179648 | tf_op jit(solution)/shard_map/all_gather | solution.py:126
  7.3 86.2 %all-gather.7.cloned.1.call-start = ((), (), s32[]{:S(2)}) async-start(), calls=%async_computation.3 | async-start | bytes 1179648 | tf_op jit(solution)/shard_map/all_gather | solution.py:125
  8.0 159.7 %all-gather.9.cloned.1.call-start = ((), (), s32[]{:S(2)}) async-start(), calls=%async_computation.4 | async-start | bytes 4718592 | tf_op jit(solution)/shard_map/all_gather | solution.py:124
  8.7 234.2 %all-gather.11.cloned.1.call-start = ((), (), s32[]{:S(2)}) async-start(), calls=%async_computation.5 | async-start | bytes 4718592 | tf_op jit(solution)/shard_map/all_gather | solution.py:127
  9.3 272.1 %all-reduce.2.cloned.1.call-start = ((), (), s32[]{:S(2)}) async-start(), calls=%async_computation.6 | async-start | bytes 2097152 | tf_op jit(solution)/shard_map/psum | solution.py:141
  95.2 76.0 %copy-start.7 = (bf16[8,256,128]{2,1,0:T(8,128)(2,1)S(1)}, bf16[8,256,128]{2,1,0:T(8,128)(2,1)}, u32[]{:S(2)}) copy-start(bf16[8,256,128]{2,1,0:T(8,128)(2,1)} %param.22) | copy-start | bytes 1572868
  171.2 1.1 copy-start.8
  247.0 35.9 %copy-start.5 = (f32[4096]{0:T(1024)S(1)}, f32[4096]{0:T(1024)}, u32[]{:S(2)}) copy-start(f32[4096]{0:T(1024)} %param.26) | copy-start | bytes 49156
  345.1 42.5 %copy-start.6 = (s32[64,2]{0,1:T(2,128)S(1)}, s32[64,2]{0,1:T(2,128)}, u32[]{:S(2)}) copy-start(s32[64,2]{0,1:T(2,128)} %param.28) | copy-start | bytes 1540
  358.0 14.1 %collective-permute-start = (bf16[8,18,3584]{2,0,1:T(8,128)(2,1)S(1)}, bf16[8,18,3584]{2,0,1:T(8,128)(2,1)S(1)}, u32[]{:S(2)}, u32[]{:S(2)}) collective-permute-start(bf16[8,18,3584]{2,0,1:T(8,128)(2,1)S(1)} %copy.60), channel_id=1, source_target_pairs={{0,8},{8,16},{16,24},{24,0},{1,9},{9,17},{17,25},{25,1},{2,10},{10... | collective-permute-start | bytes 3096584 | tf_op jit(solution)/shard_map/ppermute | solution.py:21
  372.1 1.0 copy-start.2
  373.1 14.2 %collective-permute-start.1 = (bf16[8,18,3584]{2,0,1:T(8,128)(2,1)S(1)}, bf16[8,18,3584]{2,0,1:T(8,128)(2,1)}, u32[]{:S(2)}, u32[]{:S(2)}) collective-permute-start(bf16[8,18,3584]{2,0,1:T(8,128)(2,1)S(1)} %collective-permute-done), channel_id=1, source_target_pairs={{0,8},{8,16},{16,24},{24,0},{1,9},{9,17},{17,25},{25,1},{2,10},{10... | collective-permute-start | bytes 3096584 | tf_op jit(solution)/shard_map/ppermute | solution.py:21
  387.3 14.4 %collective-permute-start.2 = (bf16[8,18,3584]{2,0,1:T(8,128)(2,1)}, bf16[8,18,3584]{2,0,1:T(8,128)(2,1)}, u32[]{:S(2)}, u32[]{:S(2)}) collective-permute-start(bf16[8,18,3584]{2,0,1:T(8,128)(2,1)} %collective-permute-done.1), channel_id=1, source_target_pairs={{0,8},{8,16},{16,24},{24,0},{1,9},{9,17},{17,25},{25,1},{2,10},{10... | collective-permute-start | bytes 3096584 | tf_op jit(solution)/shard_map/ppermute | solution.py:21
  387.7 19.3 %copy-start.3 = (bf16[8,18,3584]{2,0,1:T(8,128)(2,1)S(1)}, bf16[8,18,3584]{2,0,1:T(8,128)(2,1)}, u32[]{:S(2)}) copy-start(bf16[8,18,3584]{2,0,1:T(8,128)(2,1)} %copy-done.2) | copy-start | bytes 3096580
  432.4 14.3 %all-to-all-start.1 = ((bf16[8,18,1024]{2,1,0:T(8,128)(2,1)}), bf16[8,18,1024]{2,1,0:T(8,128)(2,1)S(1)}, u32[]{:S(2)}, u32[]{:S(2)}) async-start(bf16[8,18,1024]{2,1,0:T(8,128)(2,1)} %fusion.16), calls=%async_computation.1 | async-start | bytes 786432 | tf_op jit(solution)/shard_map/all_to_all | solution.py:163
Sparse Core Ops, SparseCore 0:
  9.5 42.8 all-gather.4
  54.5 38.8 all-gather.6
  95.6 72.1 all-gather.8
  169.6 73.2 all-gather.10
  247.1 34.2 all-reduce.1
